TPU v7x, 256 devices: a whole 4x4x8 slice. The times are simulated.
256 devices in a mesh: dp: 32 (over z, x), rows: 8 (over y, core).
Axes of the slice: x: 4, y: 4, z: 8, core: 2. Of those that a mesh axis runs over, the one named last changes fastest.
Arguments:
- token_ids: int32 [256, 128], P(('dp', 'rows')), may hold values from 0 to 8191, as said below
- upstream: bfloat16 [256, 128, 5376], P(('dp', 'rows')), may hold values from -6 to 6
- saved_rows: bfloat16 [256, 128, 5376], P(('dp', 'rows')), may hold values from -4 to 4
- norm_gain: float32 [5376], replicated, may hold values from 0.5 to 1.5
- master: float32 [8192, 5376], P('rows', 'dp'), may hold values from -6 to 6
- moment_one: float32 [8192, 5376], P('rows', 'dp'), may hold values from -4 to 4
- moment_two: float32 [8192, 5376], P('rows', 'dp'), may hold values from 0.1 to 4
Outputs:
- master_new: float32 [8192, 5376], P('rows', 'dp')
- moment_one_new: float32 [8192, 5376], P('rows', 'dp')
- moment_two_new: float32 [8192, 5376], P('rows', 'dp')
- new_rows: bfloat16 [256, 128, 5376], P(('dp', 'rows'))
Inputs may be any that keep to these rules, and one draw needn't show every extreme that they name: `token_ids`: rows v with v // 1024 = k belong to owner k. In each sequence, one owner receives exactly 32 of its tokens and every other owner at most 32.
All inputs are finite; a program needn't handle non-finite values.
Results may differ from a plain program's by a relative error of at most 0.007.
Values may be sent and summed in bfloat16 or wider, within the bound.
A program may use at most 64 MiB of HBM per device.

v0:
```python
import math

import jax
import jax.numpy as jnp
from jax import lax
from jax.sharding import PartitionSpec as P


def from_everyone(x, axis):
    copies = jnp.broadcast_to(x, (lax.axis_size(axis), *x.shape))
    return lax.all_to_all(copies, axis, split_axis=0, concat_axis=0, tiled=True)


def in_order(tiles, dim):
    dims = list(tiles.shape[1:])
    dims[dim] *= tiles.shape[0]
    return jnp.moveaxis(tiles, 0, dim).reshape(dims)


def collect(x, axis, dim):
    tiles = from_everyone(x, axis)
    return in_order(tiles, dim)


def norm_back(upstream_rows, saved, gain):
    values = saved.astype(jnp.float32)
    row_mean = jnp.mean(values, axis=-1, keepdims=True)
    centered = values - row_mean
    variance = jnp.mean(centered * centered, axis=-1, keepdims=True)
    inv_std = lax.rsqrt(variance + 1e-05)
    normed = centered * inv_std
    scaled = upstream_rows.astype(jnp.float32) * gain
    mean_scaled = jnp.mean(scaled, axis=-1, keepdims=True)
    mean_cross = jnp.mean(scaled * normed, axis=-1, keepdims=True)
    return (inv_std * (scaled - mean_scaled - normed * mean_cross)).astype(jnp.bfloat16)


def per_device(token_ids, upstream, saved_rows, norm_gain, master, moment_one, moment_two):
    owned_rows = master.shape[0]
    slice_width = master.shape[1]
    seq_tokens = token_ids.shape[1]
    group_ids = collect(token_ids, "dp", 0)
    row_input = norm_back(upstream[0], saved_rows[0], norm_gain)[None]
    slices = lax.all_to_all(row_input, "dp", split_axis=2, concat_axis=0, tiled=True)
    row_iota = lax.iota(jnp.int32, owned_rows)
    owners = lax.axis_size("rows")
    seq_count = slices.shape[0]
    capacity = seq_tokens // 4
    owner = group_ids // owned_rows
    local = group_ids - owner * owned_rows
    owner_hot = (owner[:, :, None] == lax.iota(jnp.int32, owners)[None, None, :]).astype(jnp.int32)
    before = jnp.cumsum(owner_hot, axis=1) - owner_hot
    slot_rank = jnp.sum(before * owner_hot, axis=2)
    target = owner * capacity + slot_rank
    placed = target[:, None, :] == lax.iota(jnp.int32, owners * capacity)[None, :, None]
    buckets = jnp.einsum(
        "sct,std->scd", placed.astype(jnp.bfloat16), slices, preferred_element_type=jnp.float32
    ).astype(jnp.bfloat16)
    bucket_ids = jnp.sum(jnp.where(placed, local[:, None, :] + 1, 0), axis=2) - 1
    buckets = buckets.reshape(seq_count, owners, capacity, slice_width)
    bucket_ids = bucket_ids.reshape(seq_count, owners, capacity)
    arrived, arrived_ids = (
        lax.all_to_all(buckets, "rows", split_axis=1, concat_axis=1, tiled=True),
        lax.all_to_all(bucket_ids, "rows", split_axis=1, concat_axis=1, tiled=True),
    )
    group_size = math.gcd(seq_count, 8)
    grouped_grad = arrived.reshape(
        seq_count // group_size, group_size * owners * capacity, slice_width
    )
    grouped_ids = arrived_ids.reshape(seq_count // group_size, group_size * owners * capacity)

    def add_routed(carried, group_item):
        part_grad, part_ids = group_item
        one_hot = (row_iota[:, None] == part_ids[None, :]).astype(jnp.bfloat16)
        return (carried + jnp.dot(one_hot, part_grad, preferred_element_type=jnp.float32), None)

    start_grad = jnp.zeros((owned_rows, slice_width), jnp.float32)
    row_grad, _ = lax.scan(add_routed, start_grad, (grouped_grad, grouped_ids))
    moment_one_new = 0.9 * moment_one + 0.1 * row_grad
    moment_two_new = 0.999 * moment_two + 0.001 * row_grad * row_grad
    first_fix = 1.0 - 0.9**10
    second_fix = 1.0 - 0.999**10
    update = (
        moment_one_new / first_fix / (jnp.sqrt(moment_two_new / second_fix) + 1e-08) + 0.1 * master
    )
    master_new = master - 0.05 * update
    table_slice = lax.all_gather(master_new.astype(jnp.bfloat16), "rows", axis=0, tiled=True)
    looked_up = jnp.take(table_slice, group_ids, axis=0)
    new_rows = lax.all_to_all(looked_up, "dp", split_axis=0, concat_axis=2, tiled=True)
    return (master_new, moment_one_new, moment_two_new, new_rows)


def solution(mesh):
    return jax.shard_map(
        per_device,
        mesh=mesh,
        in_specs=(
            P(("dp", "rows"), None),
            P(("dp", "rows"), None, None),
            P(("dp", "rows"), None, None),
            P(),
            P("rows", "dp"),
            P("rows", "dp"),
            P("rows", "dp"),
        ),
        out_specs=(
            P("rows", "dp"),
            P("rows", "dp"),
            P("rows", "dp"),
            P(("dp", "rows"), None, None),
        ),
        check_vma=False,
    )
```

profile of v0, /device:TPU:1, one launch (start us, length us, event | category | flops | bytes accessed | tf_op | source)
XLA Modules:
  0.0 313.8 jit_solution(17425573362878609456)
XLA Ops:
  7.2 0.0 copy-start
  7.2 0.0 copy-start.1
  7.2 0.0 copy-start.6
  7.2 1.4 broadcast_in_dim.44
  8.6 11.9 %all-to-all-start = ((s32[32,1,128]{2,1,0:T(1,128)}), s32[32,1,128]{2,1,0:T(1,128)S(1)}, u32[]{:S(2)}, u32[]{:S(2)}) async-start(s32[32,1,128]{2,1,0:T(1,128)} %broadcast_in_dim.44), calls=%async_computation | async-start | bytes 32768 | tf_op jit(solution)/shard_map/all_to_all | solution.py:11
  20.5 1.6 convert_reduce_fusion
  22.1 1.9 fusion.22
  24.0 0.0 copy-done
  24.0 0.0 copy-done.1
  24.0 0.0 copy-done.6
  24.0 0.9 fusion.17
  24.9 2.2 fusion.14
  27.1 6.3 %copy.105 = bf16[1,128,5376]{1,0,2:T(2,128)(2,1)S(1)} copy(bf16[1,128,5376]{2,1,0:T(8,128)(2,1)} %fusion.14) | data formatting | bytes 2752512 | tf_op jit(solution)/shard_map/convert_element_type | solution.py:35
  33.4 0.5 broadcast.187
  33.9 30.3 %reduce.2 = bf16[5376,128]{1,0:T(8,128)(2,1)} reduce(bf16[5376,1,128]{2,1,0:T(2,128)(2,1)S(1)} %bitcast.66, bf16[]{:T(256)} %broadcast.187), dimensions={1}, to_apply=%bitcast.56.reduce_sub_computation | reduce | bytes 2752514
  64.1 4.0 %reshape.172 = bf16[32,2,10752]{2,1,0:T(2,128)(2,1)} reshape(bf16[5376,128]{1,0:T(8,128)(2,1)} %reduce.2) | data formatting | bytes 2752512
  68.1 0.0 all-to-all-done
  68.1 9.4 %all-to-all-start.2 = ((bf16[32,2,10752]{2,1,0:T(2,128)(2,1)}), bf16[32,2,10752]{2,1,0:T(2,128)(2,1)S(1)}, u32[]{:S(2)}, u32[]{:S(2)}) async-start(bf16[32,2,10752]{2,1,0:T(2,128)(2,1)} %reshape.172), calls=%async_computation.2 | async-start | bytes 2752512 | tf_op jit(solution)/shard_map/all_to_all | solution.py:44
  77.5 0.1 copy.99
  77.6 0.1 copy.95
  77.7 3.3 %fusion.27 = s32[32,128]{0,1:T(8,128)S(1)} fusion(s32[32,128]{0,1:T(8,128)S(1)} %copy.99), kind=kOutput, calls=%fused_computation.37 | output fusion | flops 4386816 | bytes 32768 | tf_op jit(solution)/shard_map/jit(cumsum)/reduce_window_sum | solution.py:52
  81.1 0.1 fusion.32
  81.1 0.1 copy.100
  81.2 0.1 copy.102
  81.3 1.6 select_reduce_fusion
  82.9 0.1 sub.55
  83.0 0.7 reshape.170
  83.8 25.5 %all-to-all-done.2 = bf16[32,2,10752]{2,1,0:T(2,128)(2,1)S(1)} async-done(((bf16[32,2,10752]{2,1,0:T(2,128)(2,1)}), bf16[32,2,10752]{2,1,0:T(2,128)(2,1)S(1)}, u32[]{:S(2)}, u32[]{:S(2)}) %all-to-all-start.2) | async-done | bytes 1376288 | tf_op jit(solution)/shard_map/all_to_all | solution.py:44
  109.2 0.0 copy-start.2
  109.2 1.1 copy-done.2
  110.3 8.1 %all-to-all-start.1 = ((s32[8,1,1024]{2,1,0:T(1,128)}), s32[8,1,1024]{2,1,0:T(1,128)S(1)}, u32[]{:S(2)}, u32[]{:S(2)}) async-start(s32[8,1,1024]{2,1,0:T(1,128)} %reshape.170), calls=%async_computation.1 | async-start | bytes 65536 | tf_op jit(solution)/shard_map/all_to_all | solution.py:64
  118.5 7.8 %reshape.173 = bf16[5376,1,128]{2,1,0:T(2,128)(2,1)S(1)} reshape(bf16[32,2,10752]{2,1,0:T(2,128)(2,1)} %copy-done.2) | data formatting | bytes 2752512
  126.3 0.2 copy.112
  126.5 1.5 fusion.26
  128.0 4.0 %copy.106 = bf16[32,256,168]{2,1,0:T(8,128)(2,1)} copy(bf16[32,256,168]{1,2,0:T(8,128)(2,1)S(1)} %fusion.26) | data formatting | bytes 5505024 | tf_op jit(solution)/shard_map/convert_element_type | solution.py:58
  132.1 4.8 %copy.107 = bf16[32,8,32,168]{3,2,0,1:T(8,128)(2,1)} copy(bf16[32,8,32,168]{3,2,1,0:T(8,128)(2,1)} %bitcast.65) | data formatting | bytes 5505024 | tf_op jit(solution)/shard_map/reshape | solution.py:60
  136.9 0.0 all-to-all-done.1
  136.9 4.8 %all-to-all-start.3 = ((bf16[32,8,32,168]{3,2,0,1:T(8,128)(2,1)}), bf16[32,8,32,168]{3,2,0,1:T(8,128)(2,1)}, u32[]{:S(2)}, u32[]{:S(2)}) async-start(bf16[32,8,32,168]{3,2,0,1:T(8,128)(2,1)} %copy.107), calls=%async_computation.3 | async-start | bytes 8388608 | tf_op jit(solution)/shard_map/all_to_all | solution.py:63
  141.7 0.0 all-gather.2.cloned.1.call-start
  141.7 0.5 broadcast.186
  142.2 0.7 reduce.1
  142.9 0.1 reshape.171
  143.0 0.1 copy.104
  143.1 0.1 reshape.156
  143.2 47.4 %all-to-all-done.3 = bf16[32,8,32,168]{3,2,0,1:T(8,128)(2,1)} async-done(((bf16[32,8,32,168]{3,2,0,1:T(8,128)(2,1)}), bf16[32,8,32,168]{3,2,0,1:T(8,128)(2,1)}, u32[]{:S(2)}, u32[]{:S(2)}) %all-to-all-start.3) | async-done | bytes 2752544 | tf_op jit(solution)/shard_map/all_to_all | solution.py:63
  190.6 4.8 %copy.108 = bf16[32,8,32,168]{3,2,1,0:T(8,128)(2,1)} copy(bf16[32,8,32,168]{3,2,0,1:T(8,128)(2,1)} %all-to-all-done.3) | data formatting | bytes 5505024 | tf_op jit(solution)/shard_map/all_to_all | solution.py:63
  195.4 0.0 copy-start.3
  195.4 13.7 %while.11 = (s32[]{:T(128)}, f32[1024,168]{0,1:T(8,128)S(1)}, s32[4,2048]{1,0:T(4,128)S(1)}, bf16[4,2048,168]{2,1,0:T(8,128)(2,1)}, s32[]{:T(128)}, /*index=5*/s32[]{:T(128)}) while((s32[]{:T(128)}, f32[1024,168]{0,1:T(8,128)S(1)}, s32[4,2048]{1,0:T(4,128)S(1)}, bf16[4,2048,168]{2,1,0:T(8,128)(2,1)}, s32[]{:T(128)}, ...), condition=%wide.region_8.9_spmd.clone, body=%wide.region_7.8_spmd.clone.sunk | while | flops 707084288 | bytes 2450003 | solution.py:78
  195.4 3.5 %fusion.44 = f32[1024,168]{0,1:T(8,128)S(1)} fusion(s32[2048]{0:T(1024)S(1)} %bitcast.77, bf16[4,2048,168]{2,1,0:T(8,128)(2,1)} %get-tuple-element.127, s32[]{:T(128)} %get-tuple-element.118, f32[1024,168]{0,1:T(8,128)S(1)} %get-tuple-element.119, pred[]{:T(512)S(6)} %compare.19), kind=kOutput, calls=%fused_computation.5.clone.1 | convolution fusion | flops 707084288 | bytes 2433537 | tf_op jit(solution)/shard_map/while/body/eval_jaxpr/dot_general | solution.py:75
  198.9 3.3 %fusion.44 = f32[1024,168]{0,1:T(8,128)S(1)} fusion(s32[2048]{0:T(1024)S(1)} %bitcast.77, bf16[4,2048,168]{2,1,0:T(8,128)(2,1)} %get-tuple-element.127, s32[]{:T(128)} %get-tuple-element.118, f32[1024,168]{0,1:T(8,128)S(1)} %get-tuple-element.119, pred[]{:T(512)S(6)} %compare.19), kind=kOutput, calls=%fused_computation.5.clone.1 | convolution fusion | flops 707084288 | bytes 2433537 | tf_op jit(solution)/shard_map/while/body/eval_jaxpr/dot_general | solution.py:75
  202.3 3.3 %fusion.44 = f32[1024,168]{0,1:T(8,128)S(1)} fusion(s32[2048]{0:T(1024)S(1)} %bitcast.77, bf16[4,2048,168]{2,1,0:T(8,128)(2,1)} %get-tuple-element.127, s32[]{:T(128)} %get-tuple-element.118, f32[1024,168]{0,1:T(8,128)S(1)} %get-tuple-element.119, pred[]{:T(512)S(6)} %compare.19), kind=kOutput, calls=%fused_computation.5.clone.1 | convolution fusion | flops 707084288 | bytes 2433537 | tf_op jit(solution)/shard_map/while/body/eval_jaxpr/dot_general | solution.py:75
  205.7 3.3 %fusion.44 = f32[1024,168]{0,1:T(8,128)S(1)} fusion(s32[2048]{0:T(1024)S(1)} %bitcast.77, bf16[4,2048,168]{2,1,0:T(8,128)(2,1)} %get-tuple-element.127, s32[]{:T(128)} %get-tuple-element.118, f32[1024,168]{0,1:T(8,128)S(1)} %get-tuple-element.119, pred[]{:T(512)S(6)} %compare.19), kind=kOutput, calls=%fused_computation.5.clone.1 | convolution fusion | flops 707084288 | bytes 2433537 | tf_op jit(solution)/shard_map/while/body/eval_jaxpr/dot_general | solution.py:75
  209.0 0.0 copy-done.3
  209.1 0.0 copy-done.4
  209.1 0.0 copy-done.5
  209.1 1.8 fusion.38
  210.9 0.0 all-gather.2.cloned.1.call-update
  210.9 25.4 %all-gather.2.cloned.1.call-done = bf16[8192,168]{0,1:T(8,128)(2,1)} async-done(((bf16[1024,168]{0,1:T(8,128)(2,1)}), bf16[8192,168]{0,1:T(8,128)(2,1)}) %all-gather.2.cloned.1.call-update) | async-done | bytes 2752528 | tf_op jit(solution)/shard_map/all_gather | solution.py:87
  236.3 5.7 %copy.109 = bf16[8192,168]{1,0:T(8,128)(2,1)} copy(bf16[8192,168]{0,1:T(8,128)(2,1)} %all-gather.2.cloned.1.call-done) | data formatting | bytes 5505024 | tf_op jit(solution)/shard_map/all_gather | solution.py:87
  242.0 15.7 %gather_fusion = bf16[4096,168]{1,0:T(8,128)(2,1)S(1)} fusion(bf16[8192,168]{1,0:T(8,128)(2,1)} %copy.109, s32[4096]{0:T(1024)S(1)} %fusion.36), kind=kCustom, calls=%fused_computation | custom fusion | bytes 2768896 | tf_op jit(solution)/shard_map/jit(_take)/gather | solution.py:88
  257.8 2.4 copy.110
  260.2 0.1 broadcast_select_fusion
  260.4 45.1 %all_to_all.51 = bf16[32,128,168]{1,2,0:T(8,128)(2,1)S(1)} all-to-all(bf16[32,128,168]{1,2,0:T(8,128)(2,1)S(1)} %broadcast_select_fusion), channel_id=1, replica_groups=mesh['dp'=32,'rows'=8] {'dp'}, dimensions={0} | all-to-all | bytes 2752512 | tf_op jit(solution)/shard_map/all_to_all | solution.py:89
  305.4 1.5 copy.111
  (15 shorter events, 0.1 us)
Async XLA Ops:
  7.2 16.8 %copy-start = (bf16[1,128,5376]{2,1,0:T(8,128)(2,1)S(1)}, bf16[1,128,5376]{2,1,0:T(8,128)(2,1)}, u32[]{:S(2)}) copy-start(bf16[1,128,5376]{2,1,0:T(8,128)(2,1)} %param.11) | copy-start | bytes 4128772
  7.2 16.8 %copy-start.1 = (bf16[1,128,5376]{2,1,0:T(8,128)(2,1)S(1)}, bf16[1,128,5376]{2,1,0:T(8,128)(2,1)}, u32[]{:S(2)}) copy-start(bf16[1,128,5376]{2,1,0:T(8,128)(2,1)} %param.10) | copy-start | bytes 4128772
  7.2 16.8 %copy-start.6 = (f32[5376]{0:T(1024)S(1)}, f32[5376]{0:T(1024)}, u32[]{:S(2)}) copy-start(f32[5376]{0:T(1024)} %param.12) | copy-start | bytes 64516
  8.6 59.5 %all-to-all-start = ((s32[32,1,128]{2,1,0:T(1,128)}), s32[32,1,128]{2,1,0:T(1,128)S(1)}, u32[]{:S(2)}, u32[]{:S(2)}) async-start(s32[32,1,128]{2,1,0:T(1,128)} %broadcast_in_dim.44), calls=%async_computation | async-start | bytes 32768 | tf_op jit(solution)/shard_map/all_to_all | solution.py:11
  68.1 41.1 %all-to-all-start.2 = ((bf16[32,2,10752]{2,1,0:T(2,128)(2,1)}), bf16[32,2,10752]{2,1,0:T(2,128)(2,1)S(1)}, u32[]{:S(2)}, u32[]{:S(2)}) async-start(bf16[32,2,10752]{2,1,0:T(2,128)(2,1)} %reshape.172), calls=%async_computation.2 | async-start | bytes 2752512 | tf_op jit(solution)/shard_map/all_to_all | solution.py:44
  109.2 1.1 copy-start.2
  110.3 26.5 %all-to-all-start.1 = ((s32[8,1,1024]{2,1,0:T(1,128)}), s32[8,1,1024]{2,1,0:T(1,128)S(1)}, u32[]{:S(2)}, u32[]{:S(2)}) async-start(s32[8,1,1024]{2,1,0:T(1,128)} %reshape.170), calls=%async_computation.1 | async-start | bytes 65536 | tf_op jit(solution)/shard_map/all_to_all | solution.py:64
  136.9 53.7 %all-to-all-start.3 = ((bf16[32,8,32,168]{3,2,0,1:T(8,128)(2,1)}), bf16[32,8,32,168]{3,2,0,1:T(8,128)(2,1)}, u32[]{:S(2)}, u32[]{:S(2)}) async-start(bf16[32,8,32,168]{3,2,0,1:T(8,128)(2,1)} %copy.107), calls=%async_computation.3 | async-start | bytes 8388608 | tf_op jit(solution)/shard_map/all_to_all | solution.py:63
  141.7 94.6 %all-gather.2.cloned.1.call-start = ((), (), s32[]{:S(2)}) async-start(), calls=%async_computation.5 | async-start | bytes 3096576 | tf_op jit(solution)/shard_map/all_gather | solution.py:87
  195.4 13.7 %copy-start.3 = (f32[1024,168]{0,1:T(8,128)S(1)}, f32[1024,168]{0,1:T(8,128)}, u32[]{:S(2)}) copy-start(f32[1024,168]{0,1:T(8,128)} %param.13) | copy-start | bytes 2064388
  195.4 13.7 %copy-start.4 = (f32[1024,168]{0,1:T(8,128)S(1)}, f32[1024,168]{0,1:T(8,128)}, u32[]{:S(2)}) copy-start(f32[1024,168]{0,1:T(8,128)} %param.14) | copy-start | bytes 2064388
  195.4 13.7 %copy-start.5 = (f32[1024,168]{0,1:T(8,128)S(1)}, f32[1024,168]{0,1:T(8,128)}, u32[]{:S(2)}) copy-start(f32[1024,168]{0,1:T(8,128)} %param.15) | copy-start | bytes 2064388
Sparse Core Ops, SparseCore 0:
  211.0 25.2 all-gather.1
where the time goes:
time: 315 us; the launch traced here: 314 us
  waiting for transfers between devices  98.2 us (31%)
  local copies, waits for them, and re-layouts  62.4 us (20%)
  blocking collectives  45.1 us (14%)
  other arithmetic  44.5 us (14%)
  starting transfers between devices  34.2 us (11%)
  matrix products  15 us (5%)
  between operations  14.3 us (5%)
    all_to_all x1, waiting for transfers between devices, per_device(): lax.all_to_all(buckets, 'rows', split_axis=1, concat_axis=1, tiled=True)  47.4 us
    all_to_all x1, blocking collectives, per_device(): lax.all_to_all(looked_up, 'dp', split_axis=0, concat_axis=2, tiled=True)  45.1 us
    unnamed x2, other arithmetic  30.3 us
    all_to_all x1, waiting for transfers between devices, per_device(): lax.all_to_all(row_input, 'dp', split_axis=2, concat_axis=0, tiled=True)  25.5 us
    all_gather x1, waiting for transfers between devices, per_device(): lax.all_gather(master_new.astype(jnp.bfloat16), 'rows', axis=0, tiled=True)  25.4 us
    gather x2, local copies, waits for them, and re-layouts, per_device(): looked_up = jnp.take(table_slice, group_ids, axis=0)  18.2 us
    unnamed x21, local copies, waits for them, and re-layouts  15.9 us
    dot_general x4, matrix products, add_routed(): jnp.dot(one_hot, part_grad, preferred_element_type=jnp.float32)  13.5 us
  transfers between devices with their start and end apart: 5, of which 3 were waited for; matrix products, arithmetic and copies ran while one was open for 23% of the time, Pallas kernels for 0%

commit v1 on v0

v1 whole, which is shorter than its diff:
```python
import functools

import jax
import jax.numpy as jnp
from jax import lax
from jax.experimental import pallas as pl
from jax.experimental.pallas import tpu as pltpu
from jax.sharding import PartitionSpec as P

MESH = pl.DeviceIdType.MESH
BF = jnp.bfloat16
F32 = jnp.float32
LANES = 128
NZ, NX, NY, NC = 8, 4, 4, 2
NDP, NROWS = NZ * NX, NY * NC


def norm_kernel(slice_width, up_ref, saved_ref, gain_ref, y_ref, turned):
    tokens, width = up_ref.shape
    pieces = width // LANES

    def part(i):
        return pl.ds(pl.multiple_of(i * LANES, LANES), LANES)

    def scaled_of(i):
        return up_ref[:, part(i)].astype(F32) * gain_ref[:, part(i)]

    def first(i, carried):
        total, total_scaled = carried
        return total + saved_ref[:, part(i)].astype(F32), total_scaled + scaled_of(i)

    zero = jnp.zeros((tokens, LANES), F32)
    total, total_scaled = lax.fori_loop(0, pieces, first, (zero, zero), unroll=2)
    mean = jnp.sum(total, axis=1, keepdims=True) / width
    mean_scaled = jnp.sum(total_scaled, axis=1, keepdims=True) / width

    def second(i, carried):
        squares, cross = carried
        centered = saved_ref[:, part(i)].astype(F32) - mean
        return squares + centered * centered, cross + scaled_of(i) * centered

    squares, cross = lax.fori_loop(0, pieces, second, (zero, zero), unroll=2)
    variance = jnp.sum(squares, axis=1, keepdims=True) / width
    inv_std = lax.rsqrt(variance + 1e-05)
    mean_cross = jnp.sum(cross, axis=1, keepdims=True) / width * inv_std

    def third(i, _):
        normed = (saved_ref[:, part(i)].astype(F32) - mean) * inv_std
        out = inv_std * (scaled_of(i) - mean_scaled - normed * mean_cross)
        turned[part(i), :] = out.T
        return 0

    lax.fori_loop(0, pieces, third, 0, unroll=2)

    def fourth(j, _):
        rows = pl.ds(pl.multiple_of(j * slice_width, 8), slice_width)
        y_ref[j] = turned[rows, :].astype(BF)
        return 0

    lax.fori_loop(0, width // slice_width, fourth, 0)


def adam(grad, master, one, two):
    one_new = 0.9 * one + 0.1 * grad
    two_new = 0.999 * two + 0.001 * grad * grad
    first_fix = 1.0 - 0.9**10
    second_fix = 1.0 - 0.999**10
    update = one_new / first_fix / (jnp.sqrt(two_new / second_fix) + 1e-08) + 0.1 * master
    return master - 0.05 * update, one_new, two_new


GROUP = 8


def step_kernel(
    ids_ref, y_ref, m_hbm, m1_hbm, m2_hbm, grad_ref, new_ref,
    ids_all, arrived, total, pair_out, pair_in, ring_out, ring_in, table, outgoing, state,
    ids_send, ids_recv, go_send, go_recv, back_send, back_recv,
    pair_send, pair_recv, ring_send, ring_recv, tab_send, tab_recv, local_sem,
):
    d = lax.axis_index("dp")
    r = lax.axis_index("rows")
    z, x = d // NX, d % NX
    y, c = r // NC, r % NC
    owned = grad_ref.shape[1]

    def ahead(off):
        return ((z + off // NX) % NZ) * NX + (x + off % NX) % NX

    def behind(off):
        return ((z + NZ - off // NX) % NZ) * NX + (x + NX - off % NX) % NX

    def row_peer(dy, dc):
        return ((y + dy) % NY) * NC + (c + dc) % NC

    def copy(src, dst, send, recv, dp=None, rows=None):
        return pltpu.make_async_remote_copy(
            src_ref=src, dst_ref=dst, send_sem=send, recv_sem=recv,
            device_id={"dp": d if dp is None else dp, "rows": r if rows is None else rows},
            device_id_type=MESH,
        )

    barrier = pltpu.get_barrier_semaphore()

    def greet(off, _):
        pl.semaphore_signal(barrier, inc=1, device_id={"dp": ahead(off), "rows": r}, device_id_type=MESH)
        return 0

    lax.fori_loop(1, NDP, greet, 0)
    for dy in range(1, NY):
        pl.semaphore_signal(barrier, inc=1, device_id={"dp": d, "rows": row_peer(dy, 0)}, device_id_type=MESH)
    pl.semaphore_signal(barrier, inc=1, device_id={"dp": d, "rows": row_peer(0, 1)}, device_id_type=MESH)
    state_copies = [
        pltpu.make_async_copy(hbm, state.at[i], local_sem.at[i])
        for i, hbm in enumerate((m_hbm, m1_hbm, m2_hbm))
    ]
    for one in state_copies:
        one.start()
    pl.semaphore_wait(barrier, NDP - 1 + NY)

    def ids_copy(off):
        return copy(ids_ref, ids_all.at[off], ids_send.at[off], ids_recv.at[off], dp=ahead(off))

    def go_copy(off):
        return copy(y_ref.at[ahead(off)], arrived.at[off], go_send.at[off], go_recv.at[off], dp=ahead(off))

    def send_ids(off, _):
        ids_copy(off).start()
        return 0

    def send_go(off, _):
        go_copy(off).start()
        return 0

    lax.fori_loop(1, NDP, send_ids, 0)
    lax.fori_loop(1, NDP, send_go, 0)
    ids_all[0] = ids_ref[...]
    arrived[0] = y_ref[d]
    total[...] = jnp.zeros_like(total)

    def hot(group, base):
        rows = lax.broadcasted_iota(jnp.int32, (owned, LANES), 0) + base
        return jnp.concatenate(
            [(rows == ids_all[group * GROUP + k]).astype(F32).astype(BF) for k in range(GROUP)], axis=1
        )

    def go_group(group, _):
        def wait(k, _):
            off = group * GROUP + k

            @pl.when(off > 0)
            def _():
                ids_copy(off).wait_recv()
                go_copy(off).wait_recv()

            return 0

        lax.fori_loop(0, GROUP, wait, 0)
        block = jnp.concatenate([arrived[group * GROUP + k] for k in range(GROUP)], axis=1)

        def owner_step(k, _):
            total[k] += lax.dot_general(
                block, hot(group, k * owned), (((1,), (1,)), ((), ())), preferred_element_type=F32
            )
            return 0

        lax.fori_loop(0, NROWS, owner_step, 0)
        return 0

    lax.fori_loop(0, NDP // GROUP, go_group, 0)

    def pair_copy(dy):
        return copy(
            pair_out.at[dy], pair_in.at[dy], pair_send.at[dy], pair_recv.at[dy], rows=row_peer(0, 1)
        )

    for dy in (2, 1, 3, 0):
        pair_out[dy] = total[row_peer(dy, 1)].astype(BF)
        pair_copy(dy).start()

    def ring_copy(dy):
        return copy(
            ring_out.at[dy], ring_in.at[dy], ring_send.at[dy], ring_recv.at[dy], rows=row_peer(dy, 0)
        )

    for dy in (2, 1, 3):
        pair_copy(dy).wait_recv()
        ring_out[dy] = (total[row_peer(dy, 0)] + pair_in[dy].astype(F32)).astype(BF)
        ring_copy(dy).start()
    pair_copy(0).wait_recv()
    grad = total[row_peer(0, 0)] + pair_in[0].astype(F32)
    for dy in (1, 3, 2):
        ring_copy(dy).wait_recv()
        grad = grad + ring_in[dy].astype(F32)
    grad_ref[...] = grad
    for one in state_copies:
        one.wait()
    table[r] = adam(grad_ref[...], state[0], state[1], state[2])[0].astype(BF)

    def spread_copy(dy):
        return copy(table.at[r], table.at[r], tab_send.at[dy], tab_recv.at[dy], rows=row_peer(dy, 0))

    def spread_wait(dy):
        k = row_peer(NY - dy, 0)
        copy(table.at[k], table.at[k], tab_send.at[dy], tab_recv.at[dy], rows=row_peer(dy, 0)).wait_recv()

    def hand_copy(dy, dc):
        k = row_peer(NY - dy, dc)
        return copy(
            table.at[k], table.at[k], tab_send.at[NY + dy], tab_recv.at[NY + dy], rows=row_peer(0, 1)
        )

    for dy in (2, 1, 3):
        spread_copy(dy).start()
    hand_copy(0, 0).start()
    for dy in (1, 3, 2):
        spread_wait(dy)
        hand_copy(dy, 0).start()
    for dy in (0, 1, 3, 2):
        hand_copy(dy, 1).wait_recv()

    def back_copy(off):
        return copy(
            outgoing.at[off], new_ref.at[d], back_send.at[off], back_recv.at[off], dp=behind(off)
        )

    def back_wait(off):
        slot = new_ref.at[ahead(off)]
        copy(slot, slot, back_send.at[off], back_recv.at[off], dp=behind(off)).wait_recv()

    def back_group(group, _):
        def owner_step(k, picked):
            return picked + jnp.dot(table[k], hot(group, k * owned), preferred_element_type=F32)

        picked = lax.fori_loop(
            0, NROWS, owner_step, jnp.zeros((grad_ref.shape[0], GROUP * LANES), F32)
        ).astype(BF)
        for k in range(GROUP):
            outgoing[group * GROUP + k] = picked[:, k * LANES:(k + 1) * LANES]

        def send(k, _):
            off = group * GROUP + k

            @pl.when(off > 0)
            def _():
                back_copy(off).start()

            return 0

        lax.fori_loop(0, GROUP, send, 0)
        return 0

    lax.fori_loop(0, NDP // GROUP, back_group, 0)
    new_ref[d] = outgoing[0]

    def finish(off, _):
        ids_copy(off).wait_send()
        go_copy(off).wait_send()
        back_copy(off).wait_send()
        back_wait(off)
        return 0

    lax.fori_loop(1, NDP, finish, 0)
    for dy in range(NY):
        pair_copy(dy).wait_send()
        hand_copy(dy, 0).wait_send()
        if dy:
            ring_copy(dy).wait_send()
            spread_copy(dy).wait_send()


def per_device(token_ids, upstream, saved_rows, norm_gain, master, moment_one, moment_two):
    owned, width = master.shape
    tokens, features = upstream.shape[1:]
    vmem = pl.BlockSpec(memory_space=pltpu.VMEM)
    hbm = pl.BlockSpec(memory_space=pl.ANY)
    limit = 60 * 1024 * 1024
    y = pl.pallas_call(
        functools.partial(norm_kernel, width),
        out_shape=jax.ShapeDtypeStruct((NDP, width, tokens), BF),
        in_specs=[vmem] * 3,
        out_specs=vmem,
        scratch_shapes=[pltpu.VMEM((features, tokens), F32)],
        compiler_params=pltpu.CompilerParams(vmem_limit_bytes=limit),
    )(upstream[0], saved_rows[0], norm_gain[None])
    turned = (master.T, moment_one.T, moment_two.T)
    dma = pltpu.SemaphoreType.DMA
    grad, new = pl.pallas_call(
        step_kernel,
        out_shape=(
            jax.ShapeDtypeStruct((width, owned), F32),
            jax.ShapeDtypeStruct((NDP, width, tokens), BF),
        ),
        in_specs=[vmem, vmem, hbm, hbm, hbm],
        out_specs=(vmem, vmem),
        scratch_shapes=[
            pltpu.VMEM((NDP, 1, tokens), jnp.int32),
            pltpu.VMEM((NDP, width, tokens), BF),
            pltpu.VMEM((NROWS, width, owned), F32),
            pltpu.VMEM((NY, width, owned), BF),
            pltpu.VMEM((NY, width, owned), BF),
            pltpu.VMEM((NY, width, owned), BF),
            pltpu.VMEM((NY, width, owned), BF),
            pltpu.VMEM((NROWS, width, owned), BF),
            pltpu.VMEM((NDP, width, tokens), BF),
            pltpu.VMEM((3, width, owned), F32),
            dma((NDP,)), dma((NDP,)), dma((NDP,)), dma((NDP,)), dma((NDP,)), dma((NDP,)),
            dma((NY,)), dma((NY,)), dma((NY,)), dma((NY,)), dma((2 * NY,)), dma((2 * NY,)),
            dma((3,)),
        ],
        compiler_params=pltpu.CompilerParams(
            collective_id=0, has_side_effects=True, vmem_limit_bytes=limit
        ),
    )(token_ids, y, *turned)
    outs = [one.T for one in adam(grad, *turned)]
    new_rows = new.reshape(features, tokens).T[None]
    return (*outs, new_rows)


def solution(mesh):
    return jax.shard_map(
        per_device,
        mesh=mesh,
        in_specs=(
            P(("dp", "rows"), None),
            P(("dp", "rows"), None, None),
            P(("dp", "rows"), None, None),
            P(),
            P("rows", "dp"),
            P("rows", "dp"),
            P("rows", "dp"),
        ),
        out_specs=(
            P("rows", "dp"),
            P("rows", "dp"),
            P("rows", "dp"),
            P(("dp", "rows"), None, None),
        ),
        check_vma=False,
    )
```

time: 315 us -> 164 us (0.52)
  Pallas kernels: 0 us -> 157 us
  waiting for transfers between devices: 98.2 us -> 0 us
  local copies, waits for them, and re-layouts: 62.4 us -> 4.04 us
  blocking collectives: 45.1 us -> 0 us
  other arithmetic: 44.5 us -> 1.82 us
  starting transfers between devices: 34.2 us -> 0 us
  matrix products: 15 us -> 0 us
  between operations: 14.3 us -> 0.68 us
    pallas_call x0 -> x2, Pallas kernels: none -> 157 us  [the longest x1 150 us: per_device(): pl.pallas_call(step_kernel, out_shape=(jax.ShapeDtypeStruct((width, owned...]
    all_to_all x4 -> x0, waiting for transfers between devices: 72.8 us -> none  [the longest x1 47.4 us: per_device(): lax.all_to_all(buckets, 'rows', split_axis=1, concat_axis=1, tiled=True)]
    all_to_all x1 -> x0, blocking collectives: 45.1 us -> none  [per_device(): lax.all_to_all(looked_up, 'dp', split_axis=0, concat_axis=2, tiled=True)]
    all_to_all x4 -> x0, starting transfers between devices: 34.2 us -> none  [the longest x1 11.9 us: from_everyone(): return lax.all_to_all(copies, axis, split_axis=0, concat_axis=0, tiled=True)]
    unnamed x2 -> x0, other arithmetic: 30.3 us -> none
    all_gather x1 -> x0, waiting for transfers between devices: 25.4 us -> none  [per_device(): lax.all_gather(master_new.astype(jnp.bfloat16), 'rows', axis=0, tiled=True)]
    gather x2 -> x0, local copies, waits for them, and re-layouts: 18.2 us -> none  [per_device(): looked_up = jnp.take(table_slice, group_ids, axis=0)]
    unnamed x21 -> x8, local copies, waits for them, and re-layouts: 15.9 us -> 0.02 us
  transfers between devices with their start and end apart: 5 -> 0, of which waited for: 3 -> 0; matrix products, arithmetic and copies ran while one was open for 23% -> 0% of each run, Pallas kernels for 0% -> 0%
where the time goes in v1:
time: 164 us
  Pallas kernels  157 us (96%)
  local copies, waits for them, and re-layouts  4.04 us (2%)
  other arithmetic  1.82 us (1%)
    pallas_call x1, Pallas kernels, per_device(): pl.pallas_call(step_kernel, out_shape=(jax.ShapeDtypeStruct((width, owned...  150 us
    pallas_call x1, Pallas kernels, per_device(): pl.pallas_call(functools.partial(norm_kernel, width), out_shape=jax.Shape...  7.55 us

profile of v1, /device:TPU:1, one launch (start us, length us, event | category | flops | bytes accessed | tf_op | source)
XLA Modules:
  0.0 163.9 jit_solution(1276506414734371244)
XLA Ops:
  0.6 1.4 broadcast_in_dim.6.gain_ref
  2.0 7.5 %shard_map.102.y_ref = bf16[32,168,128]{2,1,0:T(8,128)(2,1)} custom-call(bf16[128,5376]{1,0:T(8,128)(2,1)} %bitcast.25, bf16[128,5376]{1,0:T(8,128)(2,1)} %bitcast.26, f32[1,5376]{1,0:T(1,128)} %broadcast_in_dim.6.gain_ref), custom_call_target="tpu_custom_call" | custom-call | tf_op jit(solution)/shard_map/pallas_call | solution.py:278
  9.5 149.8 %shard_map.103 = (f32[168,1024]{1,0:T(8,128)}, bf16[32,168,128]{2,1,0:T(8,128)(2,1)}) custom-call(s32[1,128]{1,0:T(1,128)} %ids_ref.1, bf16[32,168,128]{2,1,0:T(8,128)(2,1)} %shard_map.102.y_ref, f32[168,1024]{1,0:T(8,128)} %bitcast.20, f32[168,1024]{1,0:T(8,128)} %bitcast.21, f32[168,1024]{1,0:T(8,128)} %bitcast.22), custom_call_target="tpu_custom_call" | custom-call | tf_op jit(solution)/shard_map/pallas_call | solution.py:288
  159.3 0.0 copy-start
  159.4 0.0 copy-start.1
  159.4 0.0 copy-start.2
  159.4 0.0 copy-start.3
  159.4 2.7 %copy.11 = bf16[5376,128]{0,1:T(8,128)(2,1)} copy(bf16[5376,128]{1,0:T(8,128)(2,1)} %bitcast.24) | data formatting | bytes 2752512 | tf_op jit(solution)/shard_map/reshape | solution.py:316
  162.0 0.0 copy-done
  162.1 0.0 copy-done.1
  162.1 0.0 copy-done.2
  162.1 0.0 copy-done.3
  162.1 1.8 %fusion.2 = (f32[1024,168]{0,1:T(8,128)}, f32[1024,168]{0,1:T(8,128)}, f32[1024,168]{0,1:T(8,128)}) fusion(f32[168,1024]{1,0:T(8,128)S(1)} %copy-done.3, f32[1024,168]{0,1:T(8,128)S(1)} %copy-done.2, f32[1024,168]{0,1:T(8,128)S(1)} %copy-done.1, f32[1024,168]{0,1:T(8,128)S(1)} %copy-done), kind=kLoop, calls=%fused_computation.5 | loop fusion | flops 2580480 | bytes 4816896 | tf_op jit(solution)/shard_map/transpose | solution.py:315
Async XLA Ops:
  159.3 2.7 %copy-start = (f32[1024,168]{0,1:T(8,128)S(1)}, f32[1024,168]{0,1:T(8,128)}, u32[]{:S(2)}) copy-start(f32[1024,168]{0,1:T(8,128)} %param.11) | copy-start | bytes 2064388
  159.4 2.7 %copy-start.1 = (f32[1024,168]{0,1:T(8,128)S(1)}, f32[1024,168]{0,1:T(8,128)}, u32[]{:S(2)}) copy-start(f32[1024,168]{0,1:T(8,128)} %param.12) | copy-start | bytes 2064388
  159.4 2.7 %copy-start.2 = (f32[1024,168]{0,1:T(8,128)S(1)}, f32[1024,168]{0,1:T(8,128)}, u32[]{:S(2)}) copy-start(f32[1024,168]{0,1:T(8,128)} %param.13) | copy-start | bytes 2064388
  159.4 2.7 %copy-start.3 = (f32[168,1024]{1,0:T(8,128)S(1)}, f32[168,1024]{1,0:T(8,128)}, u32[]{:S(2)}) copy-start(f32[168,1024]{1,0:T(8,128)} %get-tuple-element.6) | copy-start | bytes 2064388

commit v2 on v1

v2 whole, which is shorter than its diff:
```python
import functools

import jax
import jax.numpy as jnp
from jax import lax
from jax.experimental import pallas as pl
from jax.experimental.pallas import tpu as pltpu
from jax.sharding import PartitionSpec as P

MESH = pl.DeviceIdType.MESH
BF = jnp.bfloat16
F32 = jnp.float32
LANES = 128
NZ, NX, NY, NC = 8, 4, 4, 2
NDP, NROWS = NZ * NX, NY * NC
CHUNKS = 3
QUARTERS = 4
PER_Q = NDP // QUARTERS
SEATS = LANES // 4
LAG_RING, LAG_ADAM, LAG_HAND, LAG_BACK = 4, 6, 8, 9
TICKS = QUARTERS * (CHUNKS - 1) + LAG_BACK + QUARTERS
NT = (((1,), (1,)), ((), ()))


def norm_back(up_ref, saved_ref, gain_ref, turned):
    tokens, width = up_ref.shape
    pieces = width // LANES

    def part(i):
        return pl.ds(pl.multiple_of(i * LANES, LANES), LANES)

    def scaled_of(i):
        return up_ref[:, part(i)].astype(F32) * gain_ref[pl.ds(i, 1), :]

    def first(i, carried):
        total, total_scaled = carried
        return total + saved_ref[:, part(i)].astype(F32), total_scaled + scaled_of(i)

    zero = jnp.zeros((tokens, LANES), F32)
    total, total_scaled = lax.fori_loop(0, pieces, first, (zero, zero), unroll=2)
    mean = jnp.sum(total, axis=1, keepdims=True) / width
    mean_scaled = jnp.sum(total_scaled, axis=1, keepdims=True) / width

    def second(i, carried):
        squares, cross = carried
        centered = saved_ref[:, part(i)].astype(F32) - mean
        return squares + centered * centered, cross + scaled_of(i) * centered

    squares, cross = lax.fori_loop(0, pieces, second, (zero, zero), unroll=2)
    variance = jnp.sum(squares, axis=1, keepdims=True) / width
    inv_std = lax.rsqrt(variance + 1e-05)
    mean_cross = jnp.sum(cross, axis=1, keepdims=True) / width * inv_std

    def third(i, _):
        normed = (saved_ref[:, part(i)].astype(F32) - mean) * inv_std
        out = inv_std * (scaled_of(i) - mean_scaled - normed * mean_cross)
        turned[part(i), :] = out.T
        return 0

    lax.fori_loop(0, pieces, third, 0, unroll=2)


def adam(grad, master, one, two):
    one_new = 0.9 * one + 0.1 * grad
    two_new = 0.999 * two + 0.001 * grad * grad
    first_fix = 1.0 - 0.9**10
    second_fix = 1.0 - 0.999**10
    update = one_new / first_fix / (jnp.sqrt(two_new / second_fix) + 1e-08) + 0.1 * master
    return master - 0.05 * update, one_new, two_new


def seat_plan(ids_ref, owned, plan_ref):
    shape = (LANES, LANES)
    ids = jnp.broadcast_to(ids_ref[...], shape).astype(F32)
    across = ids.astype(jnp.int32)
    down = ids.T.astype(jnp.int32)
    owner_across, owner_down = across // owned, down // owned
    row = lax.broadcasted_iota(jnp.int32, shape, 0)
    lane = lax.broadcasted_iota(jnp.int32, shape, 1)
    earlier = (owner_across == owner_down) & (row < lane)
    rank = jnp.sum(earlier.astype(F32), axis=0, keepdims=True)
    rank_down = jnp.broadcast_to(rank, shape).T.astype(jnp.int32)
    plan_ref[pl.ds(NROWS, 1), :] = owner_across[:1] * LANES + rank.astype(jnp.int32)
    seated = rank_down == lane % SEATS
    local = (down - owner_down * owned + 1).astype(F32)
    for k in range(NROWS):
        here = jnp.where(seated & (owner_down == k), local, 0.0)
        plan_ref[pl.ds(k, 1), :] = jnp.sum(here, axis=0, keepdims=True).astype(jnp.int32) - 1


def hot(rows, wanted):
    return (lax.broadcasted_iota(jnp.int32, (rows, LANES), 0) == wanted).astype(F32).astype(BF)


def step_kernel(
    ids_ref, up_hbm, saved_hbm, gain_ref, m_hbm, m1_hbm, m2_hbm, grad_ref, new_ref,
    up_ref, saved_ref, turned, state, plan, plans, seats, y_ref, arrived, slots, total,
    pair_out, pair_in, ring_out, ring_in, table, outgoing,
    plan_send, plan_recv, go_send, go_recv, back_send, back_recv,
    pair_send, pair_recv, ring_send, ring_recv, tab_send, tab_recv, local_sem,
):
    d = lax.axis_index("dp")
    r = lax.axis_index("rows")
    z, x = d // NX, d % NX
    y, c = r // NC, r % NC
    height, owned = grad_ref.shape[1:]

    def ahead(off):
        return ((z + off // NX) % NZ) * NX + (x + off % NX) % NX

    def behind(off):
        return ((z + NZ - off // NX) % NZ) * NX + (x + NX - off % NX) % NX

    def row_peer(dy, dc):
        return ((y + dy) % NY) * NC + (c + dc) % NC

    def copy(src, dst, send, recv, dp=None, rows=None):
        return pltpu.make_async_remote_copy(
            src_ref=src, dst_ref=dst, send_sem=send, recv_sem=recv,
            device_id={"dp": d if dp is None else dp, "rows": r if rows is None else rows},
            device_id_type=MESH,
        )

    loads = [
        pltpu.make_async_copy(hbm, ref, local_sem.at[i])
        for i, (hbm, ref) in enumerate((
            (up_hbm, up_ref), (saved_hbm, saved_ref),
            (m_hbm, state.at[0]), (m1_hbm, state.at[1]), (m2_hbm, state.at[2]),
        ))
    ]
    for load in loads:
        load.start()
    barrier = pltpu.get_barrier_semaphore()

    def greet(off, _):
        pl.semaphore_signal(barrier, inc=1, device_id={"dp": ahead(off), "rows": r}, device_id_type=MESH)
        return 0

    lax.fori_loop(1, NDP, greet, 0)
    for dy in range(1, NY):
        pl.semaphore_signal(barrier, inc=1, device_id={"dp": d, "rows": row_peer(dy, 0)}, device_id_type=MESH)
    pl.semaphore_signal(barrier, inc=1, device_id={"dp": d, "rows": row_peer(0, 1)}, device_id_type=MESH)

    def clear(i, _):
        total[i] = jnp.zeros_like(total[i])
        return 0

    lax.fori_loop(0, CHUNKS * NROWS, clear, 0)
    seat_plan(ids_ref, owned, plan)
    plans[0] = plan[...]
    for load in loads:
        load.wait()
    norm_back(up_ref, saved_ref, gain_ref, turned)
    pl.semaphore_wait(barrier, NDP - 1 + NY)

    def plan_copy(off):
        return copy(plan, plans.at[off], plan_send, plan_recv, dp=ahead(off))

    def send_plan(off, _):
        plan_copy(off).start()
        return 0

    lax.fori_loop(1, NDP, send_plan, 0)

    def fill(chunk, j):
        block = j * CHUNKS + chunk
        y_ref[block] = turned[pl.ds(pl.multiple_of(block * height, 8), height), :].astype(BF)
        return block

    def send_go(chunk):
        def send(off, _):
            block = fill(chunk, ahead(off))
            copy(
                y_ref.at[block], arrived.at[chunk * NDP + off],
                go_send, go_recv.at[chunk * QUARTERS + off // PER_Q], dp=ahead(off),
            ).start()
            return 0

        lax.fori_loop(1, NDP, send, 0)
        arrived[chunk * NDP] = turned[
            pl.ds(pl.multiple_of((d * CHUNKS + chunk) * height, 8), height), :
        ].astype(BF)

    def wait_recv(ref, sem, dp=None, rows=None):
        copy(ref, ref, sem, sem, dp=dp, rows=rows).wait_recv()

    def wait_send(ref, sem, dp=None, rows=None):
        copy(ref, ref, sem, sem, dp=dp, rows=rows).wait_send()

    send_go(0)

    def wanted_slots(q, k):
        return jnp.concatenate(
            [hot(owned, seats[q * 2 + g, pl.ds(k, 1), :]) for g in range(2)], axis=1
        )

    def wanted_seats(q, g):
        first = q * PER_Q + g * 4
        return jnp.concatenate(
            [hot(owned, plans[first + s, pl.ds(NROWS, 1), :] + s * SEATS) for s in range(4)], axis=1
        )

    def pair_copy(chunk, dy):
        i = chunk * NY + dy
        return copy(
            pair_out.at[i], pair_in.at[i], pair_send.at[i], pair_recv.at[i], rows=row_peer(0, 1)
        )

    def ring_copy(chunk, dy):
        i = chunk * NY + dy
        return copy(
            ring_out.at[i], ring_in.at[i], ring_send.at[i], ring_recv.at[i], rows=row_peer(dy, 0)
        )

    def spread_copy(chunk, dy):
        ref = table.at[chunk * NROWS + r]
        i = chunk * NROWS + dy
        return copy(ref, ref, tab_send.at[i], tab_recv.at[i], rows=row_peer(dy, 0))

    def spread_wait(chunk, dy):
        ref = table.at[chunk * NROWS + row_peer(NY - dy, 0)]
        i = chunk * NROWS + dy
        copy(ref, ref, tab_send.at[i], tab_recv.at[i], rows=row_peer(dy, 0)).wait_recv()

    def hand_copy(chunk, dy, dc):
        ref = table.at[chunk * NROWS + row_peer(NY - dy, dc)]
        i = chunk * NROWS + NY + dy
        return copy(ref, ref, tab_send.at[i], tab_recv.at[i], rows=row_peer(0, 1))

    def go_part(chunk, q):
        sem = go_recv.at[chunk * QUARTERS + q]
        start = chunk * NDP + q * PER_Q

        @pl.when(q == 0)
        def _():
            wait_recv(arrived.at[pl.ds(chunk * NDP + 1, PER_Q - 1)], sem, dp=ahead(1))

        @pl.when(q > 0)
        def _():
            wait_recv(arrived.at[pl.ds(start, PER_Q)], sem, dp=ahead(1))

        for g in range(2):
            block = jnp.concatenate([arrived[start + g * 4 + s] for s in range(4)], axis=1)
            part = lax.dot_general(
                block, wanted_seats(q, g), NT, preferred_element_type=F32
            ).astype(BF)
            for k in range(NROWS):
                slots[k, :, g * LANES:(g + 1) * LANES] = part[:, k * LANES:(k + 1) * LANES]
        for dc in (1, 0):
            for dy in (2, 1, 3, 0):
                k = row_peer(dy, dc)
                summed = total[chunk * NROWS + k] + lax.dot_general(
                    slots[k], wanted_slots(q, k), NT, preferred_element_type=F32
                )
                total[chunk * NROWS + k] = summed
                if dc:

                    @pl.when(q == QUARTERS - 1)
                    def _():
                        pair_out[chunk * NY + dy] = total[chunk * NROWS + k].astype(BF)
                        pair_copy(chunk, dy).start()

    def ring_part(chunk):
        for dy in (2, 1, 3):
            i = chunk * NY + dy
            pair_copy(chunk, dy).wait_recv()
            own = total[chunk * NROWS + row_peer(dy, 0)]
            ring_out[i] = (own + pair_in[i].astype(F32)).astype(BF)
            ring_copy(chunk, dy).start()

    def adam_part(chunk):
        pair_copy(chunk, 0).wait_recv()
        grad = total[chunk * NROWS + r] + pair_in[chunk * NY].astype(F32)
        for dy in (1, 3, 2):
            ring_copy(chunk, dy).wait_recv()
            grad = grad + ring_in[chunk * NY + dy].astype(F32)
        grad_ref[chunk] = grad
        rows = pl.ds(pl.multiple_of(chunk * height, 8), height)
        fresh = adam(grad, state[0, rows, :], state[1, rows, :], state[2, rows, :])[0]
        table[chunk * NROWS + r] = fresh.astype(BF)
        for dy in (2, 1, 3):
            spread_copy(chunk, dy).start()
        hand_copy(chunk, 0, 0).start()

    def hand_part(chunk):
        for dy in (1, 3, 2):
            spread_wait(chunk, dy)
            hand_copy(chunk, dy, 0).start()

    def back_part(chunk, q):
        @pl.when(q == 0)
        def _():
            for dy in range(NY):
                hand_copy(chunk, dy, 1).wait_recv()

        picked = [
            jnp.dot(
                table[chunk * NROWS + k], wanted_slots(q, k), preferred_element_type=F32
            ).astype(BF)
            for k in range(NROWS)
        ]
        for g in range(2):
            block = jnp.concatenate([p[:, g * LANES:(g + 1) * LANES] for p in picked], axis=1)
            part = jnp.dot(block, wanted_seats(q, g), preferred_element_type=F32).astype(BF)
            first = chunk * NDP + q * PER_Q + g * 4
            for s in range(4):
                outgoing[first + s] = part[:, s * LANES:(s + 1) * LANES]

        def send(s, _):
            off = q * PER_Q + s

            @pl.when(off > 0)
            def _():
                copy(
                    outgoing.at[chunk * NDP + off], new_ref.at[d * CHUNKS + chunk],
                    back_send, back_recv, dp=behind(off),
                ).start()

            return 0

        lax.fori_loop(0, PER_Q, send, 0)

        @pl.when(q == 0)
        def _():
            new_ref[d * CHUNKS + chunk] = outgoing[chunk * NDP]

    def tick(t, _):
        @pl.when((t % QUARTERS == 0) & (t < QUARTERS * (CHUNKS - 1)))
        def _():
            send_go(t // QUARTERS + 1)

        @pl.when(t == 0)
        def _():
            wait_recv(plans.at[pl.ds(1, NDP - 1)], plan_recv, dp=ahead(1))
            lane = lax.broadcasted_iota(jnp.int32, (NROWS, LANES), 1)
            for g in range(NDP // 4):
                merged = plans[g * 4, :NROWS, :]
                for s in range(1, 4):
                    merged = jnp.where(lane >= s * SEATS, plans[g * 4 + s, :NROWS, :], merged)
                seats[g] = merged

        @pl.when(t < QUARTERS * CHUNKS)
        def _():
            go_part(t // QUARTERS, t % QUARTERS)

        for lag, work in ((LAG_RING, ring_part), (LAG_ADAM, adam_part), (LAG_HAND, hand_part)):

            @pl.when((t >= lag) & (t % QUARTERS == lag % QUARTERS) & (t < lag + QUARTERS * CHUNKS))
            def _():
                work((t - lag) // QUARTERS)

        @pl.when(t >= LAG_BACK)
        def _():
            back_part((t - LAG_BACK) // QUARTERS, (t - LAG_BACK) % QUARTERS)

        return 0

    lax.fori_loop(0, TICKS, tick, 0)

    sent = (NDP - 1) * CHUNKS
    wait_send(plans.at[pl.ds(0, NDP - 1)], plan_send, dp=ahead(1))
    wait_send(arrived.at[pl.ds(0, sent)], go_send, dp=ahead(1))
    wait_send(outgoing.at[pl.ds(0, sent)], back_send, dp=ahead(1))

    def finish(chunk, _):
        for dy in range(NY):
            pair_copy(chunk, dy).wait_send()
            hand_copy(chunk, dy, 0).wait_send()
            if dy:
                ring_copy(chunk, dy).wait_send()
                spread_copy(chunk, dy).wait_send()
        return 0

    lax.fori_loop(0, CHUNKS, finish, 0)
    wait_recv(new_ref.at[pl.ds(0, sent)], back_recv, dp=ahead(1))


def per_device(token_ids, upstream, saved_rows, norm_gain, master, moment_one, moment_two):
    owned, width = master.shape
    tokens, features = upstream.shape[1:]
    height = width // CHUNKS
    vmem = pl.BlockSpec(memory_space=pltpu.VMEM)
    hbm = pl.BlockSpec(memory_space=pl.ANY)
    turned = (master.T, moment_one.T, moment_two.T)
    dma = pltpu.SemaphoreType.DMA
    blocks = NDP * CHUNKS
    rows_bf = lambda n: pltpu.VMEM((n, height, owned), BF)
    tokens_bf = lambda n: pltpu.VMEM((n, height, tokens), BF)
    grad, new = pl.pallas_call(
        step_kernel,
        out_shape=(
            jax.ShapeDtypeStruct((CHUNKS, height, owned), F32),
            jax.ShapeDtypeStruct((blocks, height, tokens), BF),
        ),
        in_specs=[vmem, hbm, hbm, vmem, hbm, hbm, hbm],
        out_specs=(vmem, vmem),
        scratch_shapes=[
            pltpu.VMEM((tokens, features), BF),
            pltpu.VMEM((tokens, features), BF),
            pltpu.VMEM((features, tokens), F32),
            pltpu.VMEM((3, width, owned), F32),
            pltpu.VMEM((2 * NROWS, tokens), jnp.int32),
            pltpu.VMEM((NDP, 2 * NROWS, tokens), jnp.int32),
            pltpu.VMEM((NDP // 4, NROWS, LANES), jnp.int32),
            tokens_bf(blocks),
            tokens_bf(blocks),
            pltpu.VMEM((NROWS, height, 2 * LANES), BF),
            pltpu.VMEM((CHUNKS * NROWS, height, owned), F32),
            rows_bf(CHUNKS * NY), rows_bf(CHUNKS * NY), rows_bf(CHUNKS * NY), rows_bf(CHUNKS * NY),
            rows_bf(CHUNKS * NROWS),
            tokens_bf(blocks),
            dma, dma, dma, dma((CHUNKS * QUARTERS,)), dma, dma,
            dma((CHUNKS * NY,)), dma((CHUNKS * NY,)), dma((CHUNKS * NY,)), dma((CHUNKS * NY,)),
            dma((CHUNKS * NROWS,)), dma((CHUNKS * NROWS,)),
            dma((5,)),
        ],
        compiler_params=pltpu.CompilerParams(
            collective_id=0, has_side_effects=True, vmem_limit_bytes=60 * 1024 * 1024
        ),
    )(token_ids, upstream[0], saved_rows[0], norm_gain.reshape(-1, LANES), *turned)
    outs = [one.T for one in adam(grad.reshape(width, owned), *turned)]
    new_rows = new.reshape(features, tokens).T[None]
    return (*outs, new_rows)


def solution(mesh):
    return jax.shard_map(
        per_device,
        mesh=mesh,
        in_specs=(
            P(("dp", "rows"), None),
            P(("dp", "rows"), None, None),
            P(("dp", "rows"), None, None),
            P(),
            P("rows", "dp"),
            P("rows", "dp"),
            P("rows", "dp"),
        ),
        out_specs=(
            P("rows", "dp"),
            P("rows", "dp"),
            P("rows", "dp"),
            P(("dp", "rows"), None, None),
        ),
        check_vma=False,
    )
```

time: 164 us -> 109 us (0.66)
  Pallas kernels: 157 us -> 103 us
    pallas_call x2 -> x1, Pallas kernels: 157 us -> 103 us  [per_device(): pl.pallas_call(step_kernel, out_shape=(jax.ShapeDtypeStruct((CHUNKS, heig...]
where the time goes in v2:
time: 109 us; the launch traced here: 108 us
  Pallas kernels  103 us (94%)
  local copies, waits for them, and re-layouts  2.68 us (2%)
  other arithmetic  1.65 us (2%)
    pallas_call x1, Pallas kernels, per_device(): pl.pallas_call(step_kernel, out_shape=(jax.ShapeDtypeStruct((CHUNKS, heig...  103 us
    reshape x1, local copies, waits for them, and re-layouts, per_device(): new_rows = new.reshape(features, tokens).T[None]  2.66 us

profile of v2, /device:TPU:1, one launch (start us, length us, event | category | flops | bytes accessed | tf_op | source)
XLA Modules:
  0.0 108.2 jit_solution(4908213450558035014)
XLA Ops:
  0.6 103.2 %shard_map.102 = (f32[3,56,1024]{2,1,0:T(8,128)}, bf16[96,56,128]{2,1,0:T(8,128)(2,1)}) custom-call(s32[1,128]{1,0:T(1,128)} %ids_ref.1, bf16[128,5376]{1,0:T(8,128)(2,1)} %bitcast.29, bf16[128,5376]{1,0:T(8,128)(2,1)} %bitcast.30, f32[42,128]{1,0:T(8,128)} %bitcast.35, f32[168,1024]{1,0:T(8,128)} %bitcast.26, f32[168,1024]{1,0:T(8,128)} %bitcast.27, ...), custom_call_target="tpu_custom_call" | custom-call | tf_op jit(solution)/shard_map/pallas_call | solution.py:389
  103.8 0.0 copy-start
  103.8 0.0 copy-start.1
  103.8 0.0 copy-start.2
  103.9 0.0 copy-start.3
  103.9 2.7 %copy.11 = bf16[5376,128]{0,1:T(8,128)(2,1)} copy(bf16[5376,128]{1,0:T(8,128)(2,1)} %bitcast.32) | data formatting | bytes 2752512 | tf_op jit(solution)/shard_map/reshape | solution.py:422
  106.5 0.0 copy-done
  106.5 0.0 copy-done.1
  106.5 0.0 copy-done.2
  106.5 0.0 copy-done.3
  106.6 1.6 %subtract_bitcast_fusion = (f32[1024,168]{0,1:T(8,128)}, f32[168,1024]{1,0:T(8,128)}, f32[168,1024]{1,0:T(8,128)}) fusion(f32[1024,168]{0,1:T(8,128)S(1)} %copy-done, f32[3,56,1024]{2,1,0:T(8,128)S(1)} %copy-done.3, f32[1024,168]{0,1:T(8,128)S(1)} %copy-done.1, f32[1024,168]{0,1:T(8,128)S(1)} %copy-done.2), kind=kLoop, calls=%fused_computation.4 | loop fusion | flops 2580480 | bytes 4816896 | tf_op jit(solution)/shard_map/transpose | solution.py:421
Async XLA Ops:
  103.8 2.7 %copy-start = (f32[1024,168]{0,1:T(8,128)S(1)}, f32[1024,168]{0,1:T(8,128)}, u32[]{:S(2)}) copy-start(f32[1024,168]{0,1:T(8,128)} %param.11) | copy-start | bytes 2064388
  103.8 2.7 %copy-start.1 = (f32[1024,168]{0,1:T(8,128)S(1)}, f32[1024,168]{0,1:T(8,128)}, u32[]{:S(2)}) copy-start(f32[1024,168]{0,1:T(8,128)} %param.12) | copy-start | bytes 2064388
  103.8 2.7 %copy-start.2 = (f32[1024,168]{0,1:T(8,128)S(1)}, f32[1024,168]{0,1:T(8,128)}, u32[]{:S(2)}) copy-start(f32[1024,168]{0,1:T(8,128)} %param.13) | copy-start | bytes 2064388
  103.9 2.7 %copy-start.3 = (f32[3,56,1024]{2,1,0:T(8,128)S(1)}, f32[3,56,1024]{2,1,0:T(8,128)}, u32[]{:S(2)}) copy-start(f32[3,56,1024]{2,1,0:T(8,128)} %get-tuple-element.6) | copy-start | bytes 2064388

commit v3 on v2

--- a/solution.py
+++ b/solution.py
@@ -19,7 +19,7 @@
 SEATS = LANES // 4
 LAG_RING, LAG_ADAM, LAG_HAND, LAG_BACK = 4, 6, 8, 9
 TICKS = QUARTERS * (CHUNKS - 1) + LAG_BACK + QUARTERS
-NT = (((1,), (1,)), ((), ()))
+GO_AT = 1
 
 
 def norm_back(up_ref, saved_ref, gain_ref, turned):
@@ -95,7 +95,7 @@
 def step_kernel(
     ids_ref, up_hbm, saved_hbm, gain_ref, m_hbm, m1_hbm, m2_hbm, grad_ref, new_ref,
     up_ref, saved_ref, turned, state, plan, plans, seats, y_ref, arrived, slots, total,
-    pair_out, pair_in, ring_out, ring_in, table, outgoing,
+    pair_out, pair_in, ring_out, ring_in, table, outgoing, columns,
     plan_send, plan_recv, go_send, go_recv, back_send, back_recv,
     pair_send, pair_recv, ring_send, ring_recv, tab_send, tab_recv, local_sem,
 ):
@@ -148,19 +148,19 @@
     lax.fori_loop(0, CHUNKS * NROWS, clear, 0)
     seat_plan(ids_ref, owned, plan)
     plans[0] = plan[...]
+    pl.semaphore_wait(barrier, NDP - 1 + NY)
+
+    def plan_copy(off):
+        return copy(plan, plans.at[off], plan_send, plan_recv, dp=ahead(off))
+
+    def send_plan(off, _):
+        plan_copy(off).start()
+        return 0
+
+    lax.fori_loop(1, NDP, send_plan, 0)
     for load in loads:
         load.wait()
     norm_back(up_ref, saved_ref, gain_ref, turned)
-    pl.semaphore_wait(barrier, NDP - 1 + NY)
-
-    def plan_copy(off):
-        return copy(plan, plans.at[off], plan_send, plan_recv, dp=ahead(off))
-
-    def send_plan(off, _):
-        plan_copy(off).start()
-        return 0
-
-    lax.fori_loop(1, NDP, send_plan, 0)
 
     def fill(chunk, j):
         block = j * CHUNKS + chunk
@@ -200,6 +200,22 @@
             [hot(owned, plans[first + s, pl.ds(NROWS, 1), :] + s * SEATS) for s in range(4)], axis=1
         )
 
+    def slot_columns(q, k):
+        lane = lax.broadcasted_iota(jnp.int32, (LANES, owned), 1)
+        return jnp.concatenate(
+            [(lane == columns[q * 2 + g, :, k:k + 1]).astype(F32).astype(BF) for g in range(2)], axis=0
+        )
+
+    def seat_columns(q, g):
+        lane = lax.broadcasted_iota(jnp.int32, (LANES, NROWS * LANES), 1)
+        return jnp.concatenate(
+            [
+                (lane == columns[q * 2 + g, :, NROWS + s:NROWS + s + 1]).astype(F32).astype(BF)
+                for s in range(4)
+            ],
+            axis=0,
+        )
+
     def pair_copy(chunk, dy):
         i = chunk * NY + dy
         return copy(
@@ -241,24 +257,19 @@
 
         for g in range(2):
             block = jnp.concatenate([arrived[start + g * 4 + s] for s in range(4)], axis=1)
-            part = lax.dot_general(
-                block, wanted_seats(q, g), NT, preferred_element_type=F32
-            ).astype(BF)
+            part = jnp.dot(block, seat_columns(q, g), preferred_element_type=F32).astype(BF)
             for k in range(NROWS):
                 slots[k, :, g * LANES:(g + 1) * LANES] = part[:, k * LANES:(k + 1) * LANES]
-        for dc in (1, 0):
+        for k in range(NROWS):
+            total[chunk * NROWS + k] += jnp.dot(
+                slots[k], slot_columns(q, k), preferred_element_type=F32
+            )
+
+        @pl.when(q == QUARTERS - 1)
+        def _():
             for dy in (2, 1, 3, 0):
-                k = row_peer(dy, dc)
-                summed = total[chunk * NROWS + k] + lax.dot_general(
-                    slots[k], wanted_slots(q, k), NT, preferred_element_type=F32
-                )
-                total[chunk * NROWS + k] = summed
-                if dc:
-
-                    @pl.when(q == QUARTERS - 1)
-                    def _():
-                        pair_out[chunk * NY + dy] = total[chunk * NROWS + k].astype(BF)
-                        pair_copy(chunk, dy).start()
+                pair_out[chunk * NY + dy] = total[chunk * NROWS + row_peer(dy, 1)].astype(BF)
+                pair_copy(chunk, dy).start()
 
     def ring_part(chunk):
         for dy in (2, 1, 3):
@@ -325,7 +336,7 @@
             new_ref[d * CHUNKS + chunk] = outgoing[chunk * NDP]
 
     def tick(t, _):
-        @pl.when((t % QUARTERS == 0) & (t < QUARTERS * (CHUNKS - 1)))
+        @pl.when((t % QUARTERS == GO_AT) & (t < QUARTERS * (CHUNKS - 1)))
         def _():
             send_go(t // QUARTERS + 1)
 
@@ -338,6 +349,9 @@
                 for s in range(1, 4):
                     merged = jnp.where(lane >= s * SEATS, plans[g * 4 + s, :NROWS, :], merged)
                 seats[g] = merged
+                goals = [plans[g * 4 + s, pl.ds(NROWS, 1), :] + s * SEATS for s in range(4)]
+                both = jnp.concatenate([merged] + goals + goals, axis=0).astype(F32)
+                columns[g] = both.T.astype(jnp.int32)
 
         @pl.when(t < QUARTERS * CHUNKS)
         def _():
@@ -409,6 +423,7 @@
             rows_bf(CHUNKS * NY), rows_bf(CHUNKS * NY), rows_bf(CHUNKS * NY), rows_bf(CHUNKS * NY),
             rows_bf(CHUNKS * NROWS),
             tokens_bf(blocks),
+            pltpu.VMEM((NDP // 4, LANES, 2 * NROWS), jnp.int32),
             dma, dma, dma, dma((CHUNKS * QUARTERS,)), dma, dma,
             dma((CHUNKS * NY,)), dma((CHUNKS * NY,)), dma((CHUNKS * NY,)), dma((CHUNKS * NY,)),
             dma((CHUNKS * NROWS,)), dma((CHUNKS * NROWS,)),

time: 109 us -> 102 us (0.936)
  Pallas kernels: 103 us -> 97.1 us
    pallas_call x1, Pallas kernels: 103 us -> 97.1 us  [per_device(): pl.pallas_call(step_kernel, out_shape=(jax.ShapeDtypeStruct((CHUNKS, heig...]
where the time goes in v3:
time: 102 us
  Pallas kernels  97.1 us (95%)
  local copies, waits for them, and re-layouts  2.68 us (3%)
  other arithmetic  1.65 us (2%)
    pallas_call x1, Pallas kernels, per_device(): pl.pallas_call(step_kernel, out_shape=(jax.ShapeDtypeStruct((CHUNKS, heig...  97.1 us
    reshape x1, local copies, waits for them, and re-layouts, per_device(): new_rows = new.reshape(features, tokens).T[None]  2.66 us

profile of v3, /device:TPU:1, one launch (start us, length us, event | category | flops | bytes accessed | tf_op | source)
XLA Modules:
  0.0 102.2 jit_solution(15683151572026031754)
XLA Ops:
  0.6 97.1 %shard_map.102 = (f32[3,56,1024]{2,1,0:T(8,128)}, bf16[96,56,128]{2,1,0:T(8,128)(2,1)}) custom-call(s32[1,128]{1,0:T(1,128)} %ids_ref.1, bf16[128,5376]{1,0:T(8,128)(2,1)} %bitcast.29, bf16[128,5376]{1,0:T(8,128)(2,1)} %bitcast.30, f32[42,128]{1,0:T(8,128)} %bitcast.35, f32[168,1024]{1,0:T(8,128)} %bitcast.26, f32[168,1024]{1,0:T(8,128)} %bitcast.27, ...), custom_call_target="tpu_custom_call" | custom-call | tf_op jit(solution)/shard_map/pallas_call | solution.py:403
  97.8 0.0 copy-start
  97.8 0.0 copy-start.1
  97.8 0.0 copy-start.2
  97.8 0.0 copy-start.3
  97.8 2.7 %copy.11 = bf16[5376,128]{0,1:T(8,128)(2,1)} copy(bf16[5376,128]{1,0:T(8,128)(2,1)} %bitcast.32) | data formatting | bytes 2752512 | tf_op jit(solution)/shard_map/reshape | solution.py:437
  100.5 0.0 copy-done
  100.5 0.0 copy-done.1
  100.5 0.0 copy-done.2
  100.5 0.0 copy-done.3
  100.5 1.6 %subtract_bitcast_fusion = (f32[1024,168]{0,1:T(8,128)}, f32[168,1024]{1,0:T(8,128)}, f32[168,1024]{1,0:T(8,128)}) fusion(f32[1024,168]{0,1:T(8,128)S(1)} %copy-done, f32[3,56,1024]{2,1,0:T(8,128)S(1)} %copy-done.3, f32[1024,168]{0,1:T(8,128)S(1)} %copy-done.1, f32[1024,168]{0,1:T(8,128)S(1)} %copy-done.2), kind=kLoop, calls=%fused_computation.4 | loop fusion | flops 2580480 | bytes 4816896 | tf_op jit(solution)/shard_map/transpose | solution.py:436
Async XLA Ops:
  97.8 2.7 %copy-start = (f32[1024,168]{0,1:T(8,128)S(1)}, f32[1024,168]{0,1:T(8,128)}, u32[]{:S(2)}) copy-start(f32[1024,168]{0,1:T(8,128)} %param.11) | copy-start | bytes 2064388
  97.8 2.7 %copy-start.1 = (f32[1024,168]{0,1:T(8,128)S(1)}, f32[1024,168]{0,1:T(8,128)}, u32[]{:S(2)}) copy-start(f32[1024,168]{0,1:T(8,128)} %param.12) | copy-start | bytes 2064388
  97.8 2.7 %copy-start.2 = (f32[1024,168]{0,1:T(8,128)S(1)}, f32[1024,168]{0,1:T(8,128)}, u32[]{:S(2)}) copy-start(f32[1024,168]{0,1:T(8,128)} %param.13) | copy-start | bytes 2064388
  97.8 2.7 %copy-start.3 = (f32[3,56,1024]{2,1,0:T(8,128)S(1)}, f32[3,56,1024]{2,1,0:T(8,128)}, u32[]{:S(2)}) copy-start(f32[3,56,1024]{2,1,0:T(8,128)} %get-tuple-element.6) | copy-start | bytes 2064388
